TPU v7x, 32 devices: a whole 2x2x4 slice. The times are simulated.
32 devices in a mesh: row: 8 (over z, core), col: 4 (over y, x).
Axes of the slice: x: 2, y: 2, z: 4, core: 2. Of those that a mesh axis runs over, the one named last changes fastest.
Arguments:
- roll_hidden: bfloat16 [1344, 4096], P(('row', 'col')), may hold values from -6 to 6
- roll_cotangent: bfloat16 [1344, 4096], P(('row', 'col')), may hold values from -6 to 6
- lengths: int32 [32], P(('row', 'col')), may hold values from 1 to 42, as said below
- owners: int32 [32], P(('row', 'col')), may hold values from 0 to 7, as said below
- prompts: int32 [32], P(('row', 'col')), may hold values from 0 to 3
- rewards: float32 [32], P(('row', 'col')), may hold values from -5 to 5
- gate_weight: bfloat16 [4096, 14784], P('col', 'row'), may hold values from -0.09375 to 0.09375
- up_weight: bfloat16 [4096, 14784], P('col', 'row'), may hold values from -0.09375 to 0.09375
- down_weight: bfloat16 [14784, 4096], P('row', 'col'), may hold values from -0.046875 to 0.046875
Outputs:
- grad_input: bfloat16 [1024, 4096], P('row', 'col')
- grad_gate: bfloat16 [4096, 14784], P('col', 'row')
- grad_up: bfloat16 [4096, 14784], P('col', 'row')
- grad_down: bfloat16 [14784, 4096], P('row', 'col')
Inputs may be any that keep to these rules, and one draw needn't show every extreme that they name: `owners`: each owner value names exactly 4 rows; the lengths of one owner's rows sum to at most 128, and to exactly 128 for some owner in every draw. `lengths`: some row has length 42 in every draw.
All inputs are finite; a program needn't handle non-finite values.
Results may differ from a plain program's by a relative error of at most 0.025.
Values may be sent and summed in bfloat16 or wider, within the bound.
A program may use at most 128 MiB of HBM per device.

v0:
```python
import jax
import jax.numpy as jnp
from jax import lax
from jax.sharding import PartitionSpec as P

CAPR = 128
spread_floor = 0.7


def row_weights(lengths, prompts, rewards, count_prompts):
    onehot = (prompts[:, None] == jnp.arange(count_prompts, dtype=jnp.int32)[None, :]).astype(
        jnp.float32
    )
    counts = jnp.maximum(jnp.sum(onehot, 0), 1.0)
    means = jnp.sum(onehot * rewards[:, None], 0) / counts
    centred = rewards - jnp.sum(onehot * means[None, :], 1)
    spreads = jnp.sqrt(jnp.sum(onehot * (centred * centred)[:, None], 0) / counts)
    divisor = jnp.maximum(jnp.sum(onehot * spreads[None, :], 1), spread_floor)
    return centred / divisor / lengths.astype(jnp.float32)


def row_offsets(lengths, owners):
    count = lengths.shape[0]
    places = jnp.arange(count, dtype=jnp.int32)
    earlier = (owners[None, :] == owners[:, None]) & (places[None, :] < places[:, None])
    return jnp.sum(jnp.where(earlier, lengths[None, :], 0), 1)


def source_index(lengths, owners, offsets, slot_count, capacity, total):
    count = lengths.shape[0]
    slots = jnp.arange(slot_count, dtype=jnp.int32)
    live = slots[None, :] < lengths[:, None]
    target = jnp.where(live, owners[:, None] * capacity + offsets[:, None] + slots[None, :], total)
    flat_source = slots[None, :] * count + jnp.arange(count, dtype=jnp.int32)[:, None]
    empty = jnp.full((total,), slot_count * count, jnp.int32)
    return empty.at[target.reshape(-1)].set(flat_source.reshape(-1), mode="drop")


def per_device(
    roll_hidden,
    roll_cotangent,
    lengths,
    owners,
    prompts,
    rewards,
    gate_weight,
    up_weight,
    down_weight,
):
    row_count = lax.axis_size("row")
    col_count = lax.axis_size("col")
    total_tokens = row_count * CAPR
    count_prompts = row_count * col_count // 8
    slot_count = roll_hidden.shape[0]
    width = roll_hidden.shape[1] // col_count
    local = jnp.stack(
        [
            lengths.astype(jnp.float32),
            owners.astype(jnp.float32),
            prompts.astype(jnp.float32),
            rewards,
        ],
        axis=1,
    )
    table = lax.all_gather(local, ("row", "col"), axis=0, tiled=True)
    all_lengths = table[:, 0].astype(jnp.int32)
    all_owners = table[:, 1].astype(jnp.int32)
    all_prompts = table[:, 2].astype(jnp.int32)
    weights = row_weights(all_lengths, all_prompts, table[:, 3], count_prompts)
    offsets = row_offsets(all_lengths, all_owners)
    mine = lax.dynamic_slice_in_dim(weights, lax.axis_index(("row", "col")), 1, 0)
    live = (jnp.arange(slot_count, dtype=jnp.int32) < lengths[0])[:, None]
    upstream = jnp.where(live, roll_cotangent.astype(jnp.float32) * mine[0], 0.0).astype(
        jnp.bfloat16
    )
    hidden_blocks = roll_hidden.reshape(slot_count, col_count, width)
    upstream_blocks = upstream.reshape(slot_count, col_count, width)
    hidden_cols, upstream_cols = (
        lax.all_to_all(hidden_blocks, "col", split_axis=1, concat_axis=1, tiled=True),
        lax.all_to_all(upstream_blocks, "col", split_axis=1, concat_axis=1, tiled=True),
    )
    hidden_all, upstream_all = (
        lax.all_gather(hidden_cols, "row", axis=1, tiled=True),
        lax.all_gather(upstream_cols, "row", axis=1, tiled=True),
    )
    sources = source_index(all_lengths, all_owners, offsets, slot_count, CAPR, total_tokens)
    packed = jnp.take(hidden_all.reshape(-1, width), sources, axis=0, mode="fill", fill_value=0)
    packed_grad = jnp.take(
        upstream_all.reshape(-1, width), sources, axis=0, mode="fill", fill_value=0
    )
    gate_term = jnp.dot(packed, gate_weight, preferred_element_type=jnp.float32)
    up_term = jnp.dot(packed, up_weight, preferred_element_type=jnp.float32)
    gate, upval = (
        lax.psum(gate_term.astype(jnp.bfloat16), "col").astype(jnp.float32),
        lax.psum(up_term.astype(jnp.bfloat16), "col").astype(jnp.float32),
    )
    sig = jax.nn.sigmoid(gate)
    silu = gate * sig
    hidden = (silu * upval).astype(jnp.bfloat16)
    contract_cols = (((1,), (1,)), ((), ()))
    grad_term = lax.dot_general(
        packed_grad, down_weight, contract_cols, preferred_element_type=jnp.float32
    )
    grad_hidden = lax.psum(grad_term.astype(jnp.bfloat16), "col").astype(jnp.float32)
    grad_gate_act = (grad_hidden * upval * sig * (1.0 + gate * (1.0 - sig))).astype(jnp.bfloat16)
    grad_up_act = (grad_hidden * silu).astype(jnp.bfloat16)
    contract_rows = (((0,), (0,)), ((), ()))
    grad_down = lax.dot_general(
        hidden, packed_grad, contract_rows, preferred_element_type=jnp.float32
    ).astype(jnp.bfloat16)
    grad_gate = lax.dot_general(
        packed, grad_gate_act, contract_rows, preferred_element_type=jnp.float32
    ).astype(jnp.bfloat16)
    grad_up = lax.dot_general(
        packed, grad_up_act, contract_rows, preferred_element_type=jnp.float32
    ).astype(jnp.bfloat16)
    term = lax.dot_general(
        grad_gate_act, gate_weight, contract_cols, preferred_element_type=jnp.float32
    )
    grad_input = lax.psum_scatter(
        (
            term
            + lax.dot_general(
                grad_up_act, up_weight, contract_cols, preferred_element_type=jnp.float32
            )
        ).astype(jnp.bfloat16),
        "row",
        scatter_dimension=0,
        tiled=True,
    )
    return (grad_input, grad_gate, grad_up, grad_down)


def solution(mesh):
    return jax.shard_map(
        per_device,
        mesh=mesh,
        in_specs=(
            P(("row", "col"), None),
            P(("row", "col"), None),
            P(("row", "col")),
            P(("row", "col")),
            P(("row", "col")),
            P(("row", "col")),
            P("col", "row"),
            P("col", "row"),
            P("row", "col"),
        ),
        out_specs=(P("row", "col"), P("col", "row"), P("col", "row"), P("row", "col")),
        check_vma=False,
    )
```

profile of v0, /device:TPU:0, one launch (start us, length us, event | category | flops | bytes accessed | tf_op | source)
XLA Modules:
  0.0 450.1 jit_solution(12010402054570381515)
XLA Ops:
  7.2 1.2 reshape.123
  8.5 12.2 %all_to_all.10 = bf16[42,4,1024]{2,0,1:T(8,128)(2,1)} all-to-all(bf16[42,4,1024]{2,0,1:T(8,128)(2,1)S(1)} %copy.25), channel_id=1, replica_groups=mesh['row'=8,'col'=4] {'col'}, dimensions={1} | all-to-all | bytes 688128 | tf_op jit(solution)/shard_map/all_to_all | solution.py:79
  23.5 66.8 %all-gather = f32[32,1,4]{2,1,0:T(1,128)S(1)} all-gather(f32[1,1,4]{2,1,0:T(1,128)S(1)} %maximum_bitcast_fusion), channel_id=1, replica_groups=mesh['row'=8,'col'=4] {'row','col'}, dimensions={0}, use_global_device_ids=true | all-gather | bytes 528 | tf_op jit(solution)/shard_map/all_gather | solution.py:65
  90.8 0.6 dynamic_slice.3
  91.4 1.8 select_convert_fusion
  93.5 9.5 %all_to_all.11 = bf16[42,4,1024]{2,0,1:T(8,128)(2,1)} all-to-all(bf16[42,4,1024]{2,0,1:T(8,128)(2,1)S(1)} %copy.23), channel_id=1, replica_groups=mesh['row'=8,'col'=4] {'col'}, dimensions={1} | all-to-all | bytes 688128 | tf_op jit(solution)/shard_map/all_to_all | solution.py:80
  103.6 7.6 %scatter_custom_fusion = s32[1024]{0:T(1024)S(1)} fusion(s32[1344]{0:T(1024)S(1)} %fusion.15, s32[1344]{0:T(1024)S(1)} %reshape.145, s32[]{:T(128)} %constant.14.clone.1), kind=kCustom, calls=%fused_computation.40 | custom fusion | bytes 4100 | tf_op jit(solution)/shard_map/scatter | solution.py:36
  111.3 3.4 copy.26
  114.7 5.5 %gather_fusion.1 = bf16[1024,1024]{1,0:T(8,128)(2,1)} fusion(bf16[1344,1024]{1,0:T(8,128)(2,1)S(1)} %bitcast.48, s32[1024]{0:T(1024)S(1)} %fusion.16), kind=kCustom, calls=%fused_computation.1.clone | custom fusion | bytes 4198400 | tf_op jit(solution)/shard_map/jit(_take)/gather | solution.py:87
  120.2 17.9 %all-gather.4.cloned.1.call-done = bf16[42,32,1024]{2,0,1:T(8,128)(2,1)} async-done(((bf16[42,4,1024]{2,0,1:T(8,128)(2,1)}), bf16[42,32,1024]{2,0,1:T(8,128)(2,1)}) %all-gather.4.cloned.1.call-update) | async-done | bytes 2752528 | tf_op jit(solution)/shard_map/all_gather | solution.py:84
  138.1 3.4 copy.24
  141.5 5.4 %gather_fusion = bf16[1024,1024]{1,0:T(8,128)(2,1)} fusion(bf16[1344,1024]{1,0:T(8,128)(2,1)S(1)} %bitcast.47, s32[1024]{0:T(1024)S(1)} %fusion.16), kind=kCustom, calls=%fused_computation.clone | custom fusion | bytes 4198400 | tf_op jit(solution)/shard_map/jit(_take)/gather | solution.py:88
  146.8 8.9 %convolution_convert_fusion.2 = bf16[1024,1848]{0,1:T(8,128)(2,1)} fusion(bf16[1024,1848]{0,1:T(8,128)(2,1)} %param.17, bf16[1024,1024]{1,0:T(8,128)(2,1)} %gather_fusion.1, pred[1024]{0:T(1024)(128)(4,1)S(1)} %compare_and_fusion), kind=kOutput, calls=%fused_computation.23 | convolution fusion | flops 3878477824 | bytes 9667584 | tf_op jit(solution)/shard_map/dot_general | solution.py:91
  155.8 6.3 %convolution_convert_fusion.3 = bf16[1024,1848]{0,1:T(8,128)(2,1)} fusion(bf16[1024,1848]{0,1:T(8,128)(2,1)S(1)} %copy-done.11, bf16[1024,1024]{1,0:T(8,128)(2,1)S(1)} %copy-done.6, pred[1024]{0:T(1024)(128)(4,1)S(1)} %compare_and_fusion), kind=kOutput, calls=%fused_computation.24 | convolution fusion | flops 3878477824 | bytes 9667584 | tf_op jit(solution)/shard_map/dot_general | solution.py:92
  162.2 6.3 %convolution_convert_fusion.4 = bf16[1024,1848]{0,1:T(8,128)(2,1)} fusion(bf16[1848,1024]{1,0:T(8,128)(2,1)S(1)} %copy-done.9, bf16[1024,1024]{1,0:T(8,128)(2,1)S(1)} %copy-done.7, pred[1024]{0:T(1024)(128)(4,1)S(1)} %compare_and_fusion), kind=kOutput, calls=%fused_computation.25 | convolution fusion | flops 3878477824 | bytes 9667584 | tf_op jit(solution)/shard_map/dot_general | solution.py:101
  168.6 219.0 %all-reduce.3.cloned.1.call-done = (bf16[1024,1848]{0,1:T(8,128)(2,1)}, bf16[1024,1848]{0,1:T(8,128)(2,1)}, bf16[1024,1848]{0,1:T(8,128)(2,1)}) async-done(((bf16[1024,1848]{0,1:T(8,128)(2,1)}, bf16[1024,1848]{0,1:T(8,128)(2,1)}, bf16[1024,1848]{0,1:T(8,128)(2,1)}), (bf16[1024,1848]{0,1:T(8,128)(2,1)}, bf16[1024,1848]{0,1:T(8,128)(2,1)}, bf16[1024,1848]{0,1:T(8,128)(2,1)})) %all-reduce.3.cloned.1.call-update) | async-done | bytes 11354128 | tf_op jit(solution)/shard_map/psum | solution.py:95
  387.5 6.3 %fusion.3 = bf16[1024,1848]{0,1:T(8,128)(2,1)S(1)} fusion(bf16[1024,1848]{0,1:T(8,128)(2,1)} %get-tuple-element.7, bf16[1024,1848]{0,1:T(8,128)(2,1)} %get-tuple-element.8, bf16[1024,1848]{0,1:T(8,128)(2,1)} %get-tuple-element.9), kind=kLoop, calls=%fused_computation.12 | loop fusion | flops 24600576 | bytes 15138816 | tf_op jit(solution)/shard_map/convert_element_type | solution.py:105
  393.8 1.9 copy-done.5
  395.7 4.7 %fusion.27 = f32[1024,1024]{1,0:T(8,128)S(1)} fusion(bf16[1024,1848]{0,1:T(8,128)(2,1)S(1)} %fusion.3, bf16[1024,1848]{0,1:T(8,128)(2,1)S(1)} %copy-done.10), kind=kOutput, calls=%fused_computation.66 | convolution fusion | flops 3875536896 | bytes 11763712 | tf_op jit(solution)/shard_map/dot_general | solution.py:117
  400.5 6.3 %add_convert_fusion = bf16[1024,1024]{1,0:T(8,128)(2,1)} fusion(f32[1024,1024]{1,0:T(8,128)S(1)} %fusion.27, bf16[1024,1848]{0,1:T(8,128)(2,1)S(1)} %copy-done.12, bf16[1024,1848]{0,1:T(8,128)(2,1)S(1)} %copy-done.3, bf16[1024,1848]{0,1:T(8,128)(2,1)S(1)} %copy-done.1), kind=kOutput, calls=%fused_computation.18 | convolution fusion | flops 3892772864 | bytes 17645568 | tf_op jit(solution)/shard_map/dot_general | solution.py:123
  406.8 7.9 %convolution_convert_fusion.1 = bf16[1024,1848]{0,1:T(8,128)(2,1)} fusion(bf16[1024,1848]{0,1:T(8,128)(2,1)} %copy-done.5, bf16[1024,1024]{1,0:T(8,128)(2,1)S(1)} %copy-done.6, pred[1024]{0:T(1024)(128)(4,1)S(1)} %compare_and_fusion), kind=kOutput, calls=%fused_computation.22 | convolution fusion | flops 3878477824 | bytes 9667584 | tf_op jit(solution)/shard_map/dot_general | solution.py:111
  414.7 6.4 %convolution_convert_fusion = bf16[1024,1848]{0,1:T(8,128)(2,1)} fusion(bf16[1024,1024]{1,0:T(8,128)(2,1)S(1)} %copy-done.6, pred[1024]{0:T(1024)(128)(4,1)S(1)} %compare_and_fusion, bf16[1024,1848]{0,1:T(8,128)(2,1)S(1)} %copy-done.4, bf16[1024,1848]{0,1:T(8,128)(2,1)S(1)} %copy-done.2), kind=kOutput, calls=%fused_computation.21 | convolution fusion | flops 3893616640 | bytes 13452288 | tf_op jit(solution)/shard_map/dot_general | solution.py:114
  421.2 6.4 %fusion.11 = bf16[1848,1024]{1,0:T(8,128)(2,1)} fusion(bf16[1024,1848]{0,1:T(8,128)(2,1)S(1)} %copy-done, bf16[1024,1848]{0,1:T(8,128)(2,1)S(1)} %copy-done.2, bf16[1024,1024]{1,0:T(8,128)(2,1)S(1)} %copy-done.8, pred[1024]{0:T(1024)(128)(4,1)S(1)} %compare_and_fusion), kind=kOutput, calls=%fused_computation.20 | convolution fusion | flops 3893616640 | bytes 13452288 | tf_op jit(solution)/shard_map/dot_general | solution.py:108
  427.6 16.0 %reduce-scatter.2.cloned.1.call-done = bf16[128,1024]{1,0:T(8,128)(2,1)} async-done(((bf16[1024,1024]{1,0:T(8,128)(2,1)}), bf16[128,1024]{1,0:T(8,128)(2,1)}) %reduce-scatter.2.cloned.1.call-update) | async-done | bytes 262160 | tf_op jit(solution)/shard_map/reduce_scatter | solution.py:120
  (59 shorter events, 1.9 us)
Async XLA Ops:
  7.2 104.1 %all-gather.6.cloned.1.call-start = ((), (), s32[]{:S(2)}) async-start(), calls=%async_computation.4 | async-start | bytes 3538944 | tf_op jit(solution)/shard_map/all_gather | solution.py:83
  20.8 117.3 %all-gather.4.cloned.1.call-start = ((), (), s32[]{:S(2)}) async-start(), calls=%async_computation.3 | async-start | bytes 3538944 | tf_op jit(solution)/shard_map/all_gather | solution.py:84
  103.0 284.5 %all-reduce.3.cloned.1.call-start = ((), (), s32[]{:S(2)}) async-start(), calls=%async_computation.6 | async-start | bytes 22708224 | tf_op jit(solution)/shard_map/psum | solution.py:95
  146.8 9.0 %copy-start.6 = (bf16[1024,1024]{1,0:T(8,128)(2,1)S(1)}, bf16[1024,1024]{1,0:T(8,128)(2,1)}, u32[]{:S(2)}) copy-start(bf16[1024,1024]{1,0:T(8,128)(2,1)} %gather_fusion.1) | copy-start | bytes 6291460
  146.8 9.0 %copy-start.11 = (bf16[1024,1848]{0,1:T(8,128)(2,1)S(1)}, bf16[1024,1848]{0,1:T(8,128)(2,1)}, u32[]{:S(2)}) copy-start(bf16[1024,1848]{0,1:T(8,128)(2,1)} %param.18) | copy-start | bytes 11354116
  155.8 6.4 %copy-start.7 = (bf16[1024,1024]{1,0:T(8,128)(2,1)S(1)}, bf16[1024,1024]{1,0:T(8,128)(2,1)}, u32[]{:S(2)}) copy-start(bf16[1024,1024]{1,0:T(8,128)(2,1)} %gather_fusion) | copy-start | bytes 6291460
  155.8 6.4 %copy-start.9 = (bf16[1848,1024]{1,0:T(8,128)(2,1)S(1)}, bf16[1848,1024]{1,0:T(8,128)(2,1)}, u32[]{:S(2)}) copy-start(bf16[1848,1024]{1,0:T(8,128)(2,1)} %param.19) | copy-start | bytes 11354116
  168.5 275.0 %reduce-scatter.2.cloned.1.call-start = ((), (), s32[]{:S(2)}) async-start(), calls=%async_computation.5 | async-start | bytes 2359296 | tf_op jit(solution)/shard_map/reduce_scatter | solution.py:120
  387.5 8.2 %copy-start.10 = (bf16[1024,1848]{0,1:T(8,128)(2,1)S(1)}, bf16[1024,1848]{0,1:T(8,128)(2,1)}, u32[]{:S(2)}) copy-start(bf16[1024,1848]{0,1:T(8,128)(2,1)} %param.17) | copy-start | bytes 11354116
  393.8 1.9 copy-start.5
  395.7 4.8 %copy-start.1 = (bf16[1024,1848]{0,1:T(8,128)(2,1)S(1)}, bf16[1024,1848]{0,1:T(8,128)(2,1)}, u32[]{:S(2)}) copy-start(bf16[1024,1848]{0,1:T(8,128)(2,1)} %get-tuple-element.9) | copy-start | bytes 11354116
  395.7 4.8 %copy-start.3 = (bf16[1024,1848]{0,1:T(8,128)(2,1)S(1)}, bf16[1024,1848]{0,1:T(8,128)(2,1)}, u32[]{:S(2)}) copy-start(bf16[1024,1848]{0,1:T(8,128)(2,1)} %get-tuple-element.8) | copy-start | bytes 11354116
  395.7 4.8 %copy-start.12 = (bf16[1024,1848]{0,1:T(8,128)(2,1)S(1)}, bf16[1024,1848]{0,1:T(8,128)(2,1)}, u32[]{:S(2)}) copy-start(bf16[1024,1848]{0,1:T(8,128)(2,1)} %param.18) | copy-start | bytes 11354116
  406.8 7.9 %copy-start.2 = (bf16[1024,1848]{0,1:T(8,128)(2,1)S(1)}, bf16[1024,1848]{0,1:T(8,128)(2,1)}, u32[]{:S(2)}) copy-start(bf16[1024,1848]{0,1:T(8,128)(2,1)} %get-tuple-element.9) | copy-start | bytes 11354116
  406.8 7.9 %copy-start.4 = (bf16[1024,1848]{0,1:T(8,128)(2,1)S(1)}, bf16[1024,1848]{0,1:T(8,128)(2,1)}, u32[]{:S(2)}) copy-start(bf16[1024,1848]{0,1:T(8,128)(2,1)} %get-tuple-element.8) | copy-start | bytes 11354116
  414.7 6.4 %copy-start = (bf16[1024,1848]{0,1:T(8,128)(2,1)S(1)}, bf16[1024,1848]{0,1:T(8,128)(2,1)}, u32[]{:S(2)}) copy-start(bf16[1024,1848]{0,1:T(8,128)(2,1)} %get-tuple-element.7) | copy-start | bytes 11354116
  414.7 6.4 %copy-start.8 = (bf16[1024,1024]{1,0:T(8,128)(2,1)S(1)}, bf16[1024,1024]{1,0:T(8,128)(2,1)}, u32[]{:S(2)}) copy-start(bf16[1024,1024]{1,0:T(8,128)(2,1)} %gather_fusion) | copy-start | bytes 6291460
Sparse Core Ops, SparseCore 0:
  20.9 37.9 all-gather.5
  103.1 34.8 all-gather.3
  168.6 218.8 all-reduce.2
  406.9 36.5 reduce-scatter.1
where the time goes:
time: 450 us
  waiting for transfers between devices  253 us (56%)
  blocking collectives  88.5 us (20%)
  matrix products  53.4 us (12%)
  local copies, waits for them, and re-layouts  29.7 us (7%)
  between operations  16.6 us (4%)
  other arithmetic  8.91 us (2%)
    psum x1, waiting for transfers between devices, per_device(): lax.psum(up_term.astype(jnp.bfloat16), 'col').astype(jnp.float32)  219 us
    all_gather x1, blocking collectives, per_device(): table = lax.all_gather(local, ('row', 'col'), axis=0, tiled=True)  66.8 us
    all_gather x1, waiting for transfers between devices, per_device(): lax.all_gather(upstream_cols, 'row', axis=1, tiled=True)  17.9 us
    reduce_scatter x1, waiting for transfers between devices, per_device(): lax.psum_scatter((term + lax.dot_general(grad_up_act, up_weight, contract...  16 us
    all_to_all x1, blocking collectives, per_device(): lax.all_to_all(hidden_blocks, 'col', split_axis=1, concat_axis=1, tiled=T...  12.2 us
    all_to_all x1, blocking collectives, per_device(): lax.all_to_all(upstream_blocks, 'col', split_axis=1, concat_axis=1, tiled...  9.51 us
  transfers between devices with their start and end apart: 4, of which 3 were waited for; matrix products, arithmetic and copies ran while one was open for 9% of the time, Pallas kernels for 0%

commit v1 on v0

--- a/solution.py
+++ b/solution.py
@@ -62,7 +62,8 @@
         ],
         axis=1,
     )
-    table = lax.all_gather(local, ("row", "col"), axis=0, tiled=True)
+    sent = jnp.stack([local] * lax.axis_size(("row", "col")))
+    table = jnp.concatenate(lax.all_to_all(sent, ("row", "col"), 0, 0), axis=0)
     all_lengths = table[:, 0].astype(jnp.int32)
     all_owners = table[:, 1].astype(jnp.int32)
     all_prompts = table[:, 2].astype(jnp.int32)

time: 450 us -> 397 us (0.88)
  blocking collectives: 88.5 us -> 22.6 us
  waiting for transfers between devices: 253 us -> 258 us
    all_gather x1 -> x0, blocking collectives: 66.8 us -> none  [per_device(): table = lax.all_gather(local, ('row', 'col'), axis=0, tiled=True)]
    all_to_all x0 -> x1, waiting for transfers between devices: none -> 7.09 us  [per_device(): table = jnp.concatenate(lax.all_to_all(sent, ('row', 'col'), 0, 0), axis=0)]
  transfers between devices with their start and end apart: 4 -> 5, of which waited for: 3 -> 5; matrix products, arithmetic and copies ran while one was open for 9% -> 14% of each run, Pallas kernels for 0% -> 0%
where the time goes in v1:
time: 397 us
  waiting for transfers between devices  258 us (65%)
  matrix products  55.9 us (14%)
  local copies, waits for them, and re-layouts  30.3 us (8%)
  blocking collectives  22.6 us (6%)
  between operations  16.6 us (4%)
  other arithmetic  8.92 us (2%)
  starting transfers between devices  4.48 us (1%)
    psum x1, waiting for transfers between devices, per_device(): lax.psum(up_term.astype(jnp.bfloat16), 'col').astype(jnp.float32)  219 us
    reduce_scatter x1, waiting for transfers between devices, per_device(): lax.psum_scatter((term + lax.dot_general(grad_up_act, up_weight, contract...  16 us
    all_gather x1, waiting for transfers between devices, per_device(): lax.all_gather(upstream_cols, 'row', axis=1, tiled=True)  14.6 us
    all_to_all x1, blocking collectives, per_device(): lax.all_to_all(hidden_blocks, 'col', split_axis=1, concat_axis=1, tiled=T...  12.2 us
    all_to_all x1, blocking collectives, per_device(): lax.all_to_all(upstream_blocks, 'col', split_axis=1, concat_axis=1, tiled...  10.4 us
    dot_general x1, matrix products, per_device(): gate_term = jnp.dot(packed, gate_weight, preferred_element_type=jnp.float32)  8.95 us
    dot_general x1, matrix products, per_device(): lax.dot_general(packed_grad, down_weight, contract_cols, preferred_elemen...  8.8 us
  transfers between devices with their start and end apart: 5, of which 5 were waited for; matrix products, arithmetic and copies ran while one was open for 14% of the time, Pallas kernels for 0%

profile of v1, /device:TPU:0, one launch (start us, length us, event | category | flops | bytes accessed | tf_op | source)
XLA Modules:
  0.0 397.1 jit_solution(16134206368831053686)
XLA Ops:
  8.5 12.2 %all_to_all.15 = bf16[42,4,1024]{2,0,1:T(8,128)(2,1)} all-to-all(bf16[42,4,1024]{2,0,1:T(8,128)(2,1)S(1)} %copy.24), channel_id=1, replica_groups=mesh['row'=8,'col'=4] {'col'}, dimensions={1} | all-to-all | bytes 688128 | tf_op jit(solution)/shard_map/all_to_all | solution.py:80
  24.0 4.3 %all-to-all-start = ((f32[32,1,4]{2,1,0:T(1,128)}), f32[32,1,4]{2,1,0:T(1,128)S(1)}, u32[]{:S(2)}, u32[]{:S(2)}) async-start(f32[32,1,4]{2,1,0:T(1,128)} %stack.20), calls=%async_computation | async-start | bytes 32768 | tf_op jit(solution)/shard_map/all_to_all | solution.py:66
  28.4 7.1 %all-to-all-done = f32[32,1,4]{2,1,0:T(1,128)S(1)} async-done(((f32[32,1,4]{2,1,0:T(1,128)}), f32[32,1,4]{2,1,0:T(1,128)S(1)}, u32[]{:S(2)}, u32[]{:S(2)}) %all-to-all-start) | async-done | bytes 544 | tf_op jit(solution)/shard_map/all_to_all | solution.py:66
  36.7 1.8 select_convert_fusion
  38.8 10.4 %all_to_all.16 = bf16[42,4,1024]{2,0,1:T(8,128)(2,1)} all-to-all(bf16[42,4,1024]{2,0,1:T(8,128)(2,1)S(1)} %copy.22), channel_id=1, replica_groups=mesh['row'=8,'col'=4] {'col'}, dimensions={1} | all-to-all | bytes 688128 | tf_op jit(solution)/shard_map/all_to_all | solution.py:81
  49.8 7.8 %scatter_custom_fusion = s32[1024]{0:T(1024)S(1)} fusion(s32[1344]{0:T(1024)S(1)} %fusion.15, s32[1344]{0:T(1024)S(1)} %reshape.152, s32[]{:T(128)} %constant.14.clone.1), kind=kCustom, calls=%fused_computation.40 | custom fusion | bytes 4100 | tf_op jit(solution)/shard_map/scatter | solution.py:36
  57.7 1.5 all-gather.5.cloned.1.call-done
  59.2 3.4 copy.25
  62.6 5.4 %gather_fusion.1 = bf16[1024,1024]{1,0:T(8,128)(2,1)} fusion(bf16[1344,1024]{1,0:T(8,128)(2,1)S(1)} %bitcast.48, s32[1024]{0:T(1024)S(1)} %fusion.16), kind=kCustom, calls=%fused_computation.1.clone | custom fusion | bytes 4198400 | tf_op jit(solution)/shard_map/jit(_take)/gather | solution.py:88
  68.0 9.0 %convolution_convert_fusion.2 = bf16[1024,1848]{0,1:T(8,128)(2,1)} fusion(bf16[1024,1848]{0,1:T(8,128)(2,1)} %param.17, bf16[1024,1024]{1,0:T(8,128)(2,1)} %gather_fusion.1, pred[1024]{0:T(1024)(128)(4,1)S(1)} %compare_and_fusion), kind=kOutput, calls=%fused_computation.23 | convolution fusion | flops 3878477824 | bytes 9667584 | tf_op jit(solution)/shard_map/dot_general | solution.py:92
  76.9 6.3 %convolution_convert_fusion.3 = bf16[1024,1848]{0,1:T(8,128)(2,1)} fusion(bf16[1024,1848]{0,1:T(8,128)(2,1)S(1)} %copy-done.10, bf16[1024,1024]{1,0:T(8,128)(2,1)S(1)} %copy-done.6, pred[1024]{0:T(1024)(128)(4,1)S(1)} %compare_and_fusion), kind=kOutput, calls=%fused_computation.24 | convolution fusion | flops 3878477824 | bytes 9667584 | tf_op jit(solution)/shard_map/dot_general | solution.py:93
  83.2 14.6 %all-gather.3.cloned.1.call-done = bf16[42,32,1024]{2,0,1:T(8,128)(2,1)} async-done(((bf16[42,4,1024]{2,0,1:T(8,128)(2,1)}), bf16[42,32,1024]{2,0,1:T(8,128)(2,1)}) %all-gather.3.cloned.1.call-update) | async-done | bytes 2752528 | tf_op jit(solution)/shard_map/all_gather | solution.py:85
  97.9 3.4 copy.23
  101.3 5.4 %gather_fusion = bf16[1024,1024]{1,0:T(8,128)(2,1)} fusion(bf16[1344,1024]{1,0:T(8,128)(2,1)S(1)} %bitcast.47, s32[1024]{0:T(1024)S(1)} %fusion.16), kind=kCustom, calls=%fused_computation.clone | custom fusion | bytes 4198400 | tf_op jit(solution)/shard_map/jit(_take)/gather | solution.py:89
  106.6 8.8 %convolution_convert_fusion.4 = bf16[1024,1848]{0,1:T(8,128)(2,1)} fusion(bf16[1848,1024]{1,0:T(8,128)(2,1)} %param.19, bf16[1024,1024]{1,0:T(8,128)(2,1)} %gather_fusion, pred[1024]{0:T(1024)(128)(4,1)S(1)} %compare_and_fusion), kind=kOutput, calls=%fused_computation.25 | convolution fusion | flops 3878477824 | bytes 9667584 | tf_op jit(solution)/shard_map/dot_general | solution.py:102
  115.5 219.0 %all-reduce.3.cloned.1.call-done = (bf16[1024,1848]{0,1:T(8,128)(2,1)}, bf16[1024,1848]{0,1:T(8,128)(2,1)}, bf16[1024,1848]{0,1:T(8,128)(2,1)}) async-done(((bf16[1024,1848]{0,1:T(8,128)(2,1)}, bf16[1024,1848]{0,1:T(8,128)(2,1)}, bf16[1024,1848]{0,1:T(8,128)(2,1)}), (bf16[1024,1848]{0,1:T(8,128)(2,1)}, bf16[1024,1848]{0,1:T(8,128)(2,1)}, bf16[1024,1848]{0,1:T(8,128)(2,1)})) %all-reduce.3.cloned.1.call-update) | async-done | bytes 11354128 | tf_op jit(solution)/shard_map/psum | solution.py:96
  334.5 6.3 %fusion.3 = bf16[1024,1848]{0,1:T(8,128)(2,1)S(1)} fusion(bf16[1024,1848]{0,1:T(8,128)(2,1)} %get-tuple-element.7, bf16[1024,1848]{0,1:T(8,128)(2,1)} %get-tuple-element.8, bf16[1024,1848]{0,1:T(8,128)(2,1)} %get-tuple-element.9), kind=kLoop, calls=%fused_computation.12 | loop fusion | flops 24600576 | bytes 15138816 | tf_op jit(solution)/shard_map/convert_element_type | solution.py:106
  340.8 1.9 copy-done.5
  342.7 4.7 %fusion.27 = f32[1024,1024]{1,0:T(8,128)S(1)} fusion(bf16[1024,1848]{0,1:T(8,128)(2,1)S(1)} %fusion.3, bf16[1024,1848]{0,1:T(8,128)(2,1)S(1)} %copy-done.9), kind=kOutput, calls=%fused_computation.66 | convolution fusion | flops 3875536896 | bytes 11763712 | tf_op jit(solution)/shard_map/dot_general | solution.py:118
  347.4 6.3 %add_convert_fusion = bf16[1024,1024]{1,0:T(8,128)(2,1)} fusion(f32[1024,1024]{1,0:T(8,128)S(1)} %fusion.27, bf16[1024,1848]{0,1:T(8,128)(2,1)S(1)} %copy-done.11, bf16[1024,1848]{0,1:T(8,128)(2,1)S(1)} %copy-done.3, bf16[1024,1848]{0,1:T(8,128)(2,1)S(1)} %copy-done.1), kind=kOutput, calls=%fused_computation.18 | convolution fusion | flops 3892772864 | bytes 17645568 | tf_op jit(solution)/shard_map/dot_general | solution.py:124
  353.8 7.9 %convolution_convert_fusion.1 = bf16[1024,1848]{0,1:T(8,128)(2,1)} fusion(bf16[1024,1848]{0,1:T(8,128)(2,1)} %copy-done.5, bf16[1024,1024]{1,0:T(8,128)(2,1)S(1)} %copy-done.7, pred[1024]{0:T(1024)(128)(4,1)S(1)} %compare_and_fusion), kind=kOutput, calls=%fused_computation.22 | convolution fusion | flops 3878477824 | bytes 9667584 | tf_op jit(solution)/shard_map/dot_general | solution.py:112
  361.7 6.4 %convolution_convert_fusion = bf16[1024,1848]{0,1:T(8,128)(2,1)} fusion(bf16[1024,1024]{1,0:T(8,128)(2,1)S(1)} %copy-done.7, pred[1024]{0:T(1024)(128)(4,1)S(1)} %compare_and_fusion, bf16[1024,1848]{0,1:T(8,128)(2,1)S(1)} %copy-done.4, bf16[1024,1848]{0,1:T(8,128)(2,1)S(1)} %copy-done.2), kind=kOutput, calls=%fused_computation.21 | convolution fusion | flops 3893616640 | bytes 13452288 | tf_op jit(solution)/shard_map/dot_general | solution.py:115
  368.2 6.4 %fusion.11 = bf16[1848,1024]{1,0:T(8,128)(2,1)} fusion(bf16[1024,1848]{0,1:T(8,128)(2,1)S(1)} %copy-done, bf16[1024,1848]{0,1:T(8,128)(2,1)S(1)} %copy-done.2, bf16[1024,1024]{1,0:T(8,128)(2,1)S(1)} %copy-done.8, pred[1024]{0:T(1024)(128)(4,1)S(1)} %compare_and_fusion), kind=kOutput, calls=%fused_computation.20 | convolution fusion | flops 3893616640 | bytes 13452288 | tf_op jit(solution)/shard_map/dot_general | solution.py:109
  374.6 16.0 %reduce-scatter.2.cloned.1.call-done = bf16[128,1024]{1,0:T(8,128)(2,1)} async-done(((bf16[1024,1024]{1,0:T(8,128)(2,1)}), bf16[128,1024]{1,0:T(8,128)(2,1)}) %reduce-scatter.2.cloned.1.call-update) | async-done | bytes 262160 | tf_op jit(solution)/shard_map/reduce_scatter | solution.py:121
  (59 shorter events, 4.3 us)
Async XLA Ops:
  7.2 52.0 %all-gather.5.cloned.1.call-start = ((), (), s32[]{:S(2)}) async-start(), calls=%async_computation.5 | async-start | bytes 3538944 | tf_op jit(solution)/shard_map/all_gather | solution.py:84
  24.0 11.5 %all-to-all-start = ((f32[32,1,4]{2,1,0:T(1,128)}), f32[32,1,4]{2,1,0:T(1,128)S(1)}, u32[]{:S(2)}, u32[]{:S(2)}) async-start(f32[32,1,4]{2,1,0:T(1,128)} %stack.20), calls=%async_computation | async-start | bytes 32768 | tf_op jit(solution)/shard_map/all_to_all | solution.py:66
  28.4 69.5 %all-gather.3.cloned.1.call-start = ((), (), s32[]{:S(2)}) async-start(), calls=%async_computation.4 | async-start | bytes 3538944 | tf_op jit(solution)/shard_map/all_gather | solution.py:85
  49.2 285.3 %all-reduce.3.cloned.1.call-start = ((), (), s32[]{:S(2)}) async-start(), calls=%async_computation.7 | async-start | bytes 22708224 | tf_op jit(solution)/shard_map/psum | solution.py:96
  68.0 9.0 %copy-start.6 = (bf16[1024,1024]{1,0:T(8,128)(2,1)S(1)}, bf16[1024,1024]{1,0:T(8,128)(2,1)}, u32[]{:S(2)}) copy-start(bf16[1024,1024]{1,0:T(8,128)(2,1)} %gather_fusion.1) | copy-start | bytes 6291460
  68.0 9.0 %copy-start.10 = (bf16[1024,1848]{0,1:T(8,128)(2,1)S(1)}, bf16[1024,1848]{0,1:T(8,128)(2,1)}, u32[]{:S(2)}) copy-start(bf16[1024,1848]{0,1:T(8,128)(2,1)} %param.18) | copy-start | bytes 11354116
  115.5 275.1 %reduce-scatter.2.cloned.1.call-start = ((), (), s32[]{:S(2)}) async-start(), calls=%async_computation.6 | async-start | bytes 2359296 | tf_op jit(solution)/shard_map/reduce_scatter | solution.py:121
  334.5 8.2 %copy-start.9 = (bf16[1024,1848]{0,1:T(8,128)(2,1)S(1)}, bf16[1024,1848]{0,1:T(8,128)(2,1)}, u32[]{:S(2)}) copy-start(bf16[1024,1848]{0,1:T(8,128)(2,1)} %param.17) | copy-start | bytes 11354116
  340.8 1.9 copy-start.5
  342.6 4.8 %copy-start.1 = (bf16[1024,1848]{0,1:T(8,128)(2,1)S(1)}, bf16[1024,1848]{0,1:T(8,128)(2,1)}, u32[]{:S(2)}) copy-start(bf16[1024,1848]{0,1:T(8,128)(2,1)} %get-tuple-element.9) | copy-start | bytes 11354116
  342.6 4.8 %copy-start.3 = (bf16[1024,1848]{0,1:T(8,128)(2,1)S(1)}, bf16[1024,1848]{0,1:T(8,128)(2,1)}, u32[]{:S(2)}) copy-start(bf16[1024,1848]{0,1:T(8,128)(2,1)} %get-tuple-element.8) | copy-start | bytes 11354116
  342.6 4.8 %copy-start.11 = (bf16[1024,1848]{0,1:T(8,128)(2,1)S(1)}, bf16[1024,1848]{0,1:T(8,128)(2,1)}, u32[]{:S(2)}) copy-start(bf16[1024,1848]{0,1:T(8,128)(2,1)} %param.18) | copy-start | bytes 11354116
  347.4 6.4 %copy-start.7 = (bf16[1024,1024]{1,0:T(8,128)(2,1)S(1)}, bf16[1024,1024]{1,0:T(8,128)(2,1)}, u32[]{:S(2)}) copy-start(bf16[1024,1024]{1,0:T(8,128)(2,1)} %gather_fusion.1) | copy-start | bytes 6291460
  353.8 7.9 %copy-start.2 = (bf16[1024,1848]{0,1:T(8,128)(2,1)S(1)}, bf16[1024,1848]{0,1:T(8,128)(2,1)}, u32[]{:S(2)}) copy-start(bf16[1024,1848]{0,1:T(8,128)(2,1)} %get-tuple-element.9) | copy-start | bytes 11354116
  353.8 7.9 %copy-start.4 = (bf16[1024,1848]{0,1:T(8,128)(2,1)S(1)}, bf16[1024,1848]{0,1:T(8,128)(2,1)}, u32[]{:S(2)}) copy-start(bf16[1024,1848]{0,1:T(8,128)(2,1)} %get-tuple-element.8) | copy-start | bytes 11354116
  361.7 6.5 %copy-start = (bf16[1024,1848]{0,1:T(8,128)(2,1)S(1)}, bf16[1024,1848]{0,1:T(8,128)(2,1)}, u32[]{:S(2)}) copy-start(bf16[1024,1848]{0,1:T(8,128)(2,1)} %get-tuple-element.7) | copy-start | bytes 11354116
  361.7 6.4 %copy-start.8 = (bf16[1024,1024]{1,0:T(8,128)(2,1)S(1)}, bf16[1024,1024]{1,0:T(8,128)(2,1)}, u32[]{:S(2)}) copy-start(bf16[1024,1024]{1,0:T(8,128)(2,1)} %gather_fusion) | copy-start | bytes 6291460
Sparse Core Ops, SparseCore 0:
  20.9 38.2 all-gather.4
  60.8 37.0 all-gather.2
  115.6 218.8 all-reduce.2
  353.9 36.5 reduce-scatter.1
